TPU v7x, 512 devices: a whole 4x8x8 slice. The times are simulated.
512 devices in a mesh: ctx: 32 (over y, x), head: 16 (over z, core).
Axes of the slice: x: 4, y: 8, z: 8, core: 2. Of those that a mesh axis runs over, the one named last changes fastest.
Arguments:
- activations: bfloat16 [8192, 16384], P('ctx'), may hold values from -6 to 6
- w_query: bfloat16 [16384, 2048], P('ctx', 'head'), may hold values from -0.046875 to 0.046875
- w_keyval: bfloat16 [16384, 256], P('ctx', 'head'), may hold values from -0.046875 to 0.046875
- f_query: bfloat16 [16, 128, 128], P('head'), may hold values from -1 to 1
- f_key: bfloat16 [128, 128], replicated, may hold values from -1 to 1
- w_out: bfloat16 [2048, 16384], P('ctx', 'head'), may hold values from -0.75 to 0.75
Outputs:
- sublayer_out: bfloat16 [8192, 16384], P('ctx', 'head')
All inputs are finite; a program needn't handle non-finite values.
Results may differ from a plain program's by a relative error of at most 0.0086.
Values may be sent and summed in bfloat16 or wider, within the bound.
A program may use at most 64 MiB of HBM per device.

v0:
```python
import math
import jax
import jax.numpy as jnp
from jax import lax
from jax.sharding import PartitionSpec as P

WINDOW = 64


def from_behind(array, axis, by):
    size = lax.axis_size(axis)
    pairs = [(i, i + by) for i in range(size) if 0 <= i + by < size]
    return lax.ppermute(array, axis, pairs)


def prefix(array, axis, combine, identity):
    size, mine = (lax.axis_size(axis), lax.axis_index(axis))
    everything = jax.tree.map(
        lambda part, kind: lax.all_gather(part.astype(kind), axis),
        array,
        jax.tree.map(lambda a: jnp.bfloat16 if a.dtype == jnp.float32 else a.dtype, array),
    )
    start = jax.tree.map(
        lambda part, zero: jnp.broadcast_to(jnp.asarray(zero, part.dtype), part.shape),
        array,
        identity,
    )

    def step(k, before):
        reached = k < mine
        new = combine(
            before, jax.tree.map(lambda part, own: part[k].astype(own.dtype), everything, array)
        )
        return jax.tree.map(lambda a, b: jnp.where(reached, a, b), new, before)

    return lax.fori_loop(0, size, step, start)


def normalized(logits):
    rising = jnp.exp(logits)
    falling = jnp.exp(-logits)
    rising = rising / jnp.sum(rising, axis=-1, keepdims=True)
    falling = falling / jnp.sum(falling, axis=-1, keepdims=True)
    return jnp.concatenate([rising, falling], axis=-1).astype(jnp.bfloat16)


def state_of(features, values):
    matrix = jnp.einsum("nf,nc->fc", features, values, preferred_element_type=jnp.float32)
    totals = jnp.sum(features.astype(jnp.float32), axis=0)
    return (matrix, totals)


def add_states(earlier, later):
    return (earlier[0] + later[0], earlier[1] + later[1])


def per_device(activations, w_query, w_keyval, f_query, f_key, w_out):
    length = activations.shape[0]
    head_width = f_key.shape[0]
    local_heads = f_query.shape[0]
    columns = activations
    query_sum = jnp.dot(
        columns,
        lax.all_gather(w_query, "ctx", axis=0, tiled=True),
        preferred_element_type=jnp.float32,
    )
    pair_sum = jnp.dot(
        columns,
        lax.all_gather(w_keyval, "ctx", axis=0, tiled=True),
        preferred_element_type=jnp.float32,
    )
    queries = query_sum.astype(jnp.bfloat16)
    keyval = lax.all_gather(pair_sum.astype(jnp.bfloat16), "head", axis=1, tiled=True)
    border = from_behind(keyval[length - WINDOW :], "ctx", 1)
    extended = jnp.concatenate([border, keyval], axis=0)
    ext_keys = extended[:, :head_width]
    ext_vals = extended[:, head_width:]
    first_pos = lax.axis_index("ctx") * length - WINDOW
    present = first_pos + jnp.arange(length + WINDOW) >= 0
    ext_feats = normalized(jnp.dot(ext_keys, f_key, preferred_element_type=jnp.float32))
    ext_feats = jnp.where(present[:, None], ext_feats, jnp.zeros_like(ext_feats))
    contribution = state_of(ext_feats[:length], ext_vals[:length])
    identity = (
        jnp.zeros((2 * head_width, head_width), jnp.float32),
        jnp.zeros((2 * head_width,), jnp.float32),
    )
    matrix, totals = prefix(contribution, "ctx", add_states, identity)
    query_heads = queries.reshape(length, local_heads, head_width)
    query_feats = normalized(
        jnp.einsum("thc,hcf->htf", query_heads, f_query, preferred_element_type=jnp.float32)
    )
    offsets = jnp.arange(length)[:, None] + WINDOW - jnp.arange(length + WINDOW)[None, :]
    inside = (offsets >= 0) & (offsets < WINDOW) & present[None, :]
    beyond = (offsets >= WINDOW) & present[None, :]
    scale = 1.0 / math.sqrt(head_width)
    scores = (
        jnp.einsum("thc,kc->htk", query_heads, ext_keys, preferred_element_type=jnp.float32) * scale
    )
    near_w = jnp.where(inside[None], jnp.exp(scores), 0.0)
    far_w = jnp.where(
        beyond[None],
        jnp.einsum("htf,kf->htk", query_feats, ext_feats, preferred_element_type=jnp.float32),
        0.0,
    )
    weights = near_w + far_w
    feats_wide = query_feats.astype(jnp.float32)
    numerator = jnp.einsum(
        "htk,kc->htc", weights, ext_vals.astype(jnp.float32), precision=lax.Precision.HIGHEST
    )
    numerator = numerator + jnp.einsum(
        "htf,fc->htc", feats_wide, matrix, precision=lax.Precision.HIGHEST
    )
    denominator = jnp.sum(weights, axis=-1) + jnp.einsum(
        "htf,f->ht", feats_wide, totals, precision=lax.Precision.HIGHEST
    )
    attn_heads = (numerator / denominator[..., None]).astype(jnp.bfloat16)
    attn_rows = jnp.transpose(attn_heads, (1, 0, 2)).reshape(length, local_heads * head_width)
    all_heads = lax.all_gather(attn_rows, "head", axis=1, tiled=True)
    columns = all_heads
    projected = jnp.dot(
        columns,
        lax.all_gather(w_out, "ctx", axis=0, tiled=True),
        preferred_element_type=jnp.float32,
    )
    return projected.astype(jnp.bfloat16)


def solution(mesh):
    in_specs = (
        P("ctx", None),
        P("ctx", "head"),
        P("ctx", "head"),
        P("head", None, None),
        P(),
        P("ctx", "head"),
    )
    out_specs = P("ctx", "head")
    return jax.shard_map(
        per_device, mesh=mesh, in_specs=in_specs, out_specs=out_specs, check_vma=False
    )
```

profile of v0, /device:TPU:1, one launch (start us, length us, event | category | flops | bytes accessed | tf_op | source)
XLA Modules:
  0.0 402.4 jit_solution(3140013990136511824)
XLA Ops:
  6.5 39.9 %all_gather.27 = bf16[16384,16]{0,1:T(8,128)(2,1)S(1)} all-gather(bf16[512,16]{0,1:T(8,128)(2,1)} %param.10), channel_id=1, replica_groups=mesh['ctx'=32,'head'=16] {'ctx'}, dimensions={0}, use_global_device_ids=true | all-gather | bytes 540672 | tf_op jit(solution)/shard_map/all_gather | solution.py:69
  46.5 5.6 %convolution_convert_fusion.3 = bf16[256,16]{0,1:T(8,128)(2,1)S(1)} fusion(bf16[256,16384]{1,0:T(8,128)(2,1)} %param.8, bf16[16384,16]{0,1:T(8,128)(2,1)S(1)} %all_gather.27), kind=kOutput, calls=%fused_computation.16 | convolution fusion | flops 134221824 | bytes 8921088 | tf_op jit(solution)/shard_map/dot_general | solution.py:67
  52.1 35.5 %all_gather.28 = bf16[256,256]{0,1:T(8,128)(2,1)S(1)} all-gather(bf16[256,16]{0,1:T(8,128)(2,1)S(1)} %convolution_convert_fusion.3), channel_id=1, replica_groups=mesh['ctx'=32,'head'=16] {'head'}, dimensions={1}, use_global_device_ids=true | all-gather | bytes 139264 | tf_op jit(solution)/shard_map/all_gather | solution.py:73
  87.7 2.4 collective-permute-start
  90.1 1.3 collective-permute-done
  92.2 0.9 convolution_convert_fusion.1
  93.2 0.7 all-gather.8.cloned.1.call-update
  94.7 35.3 %all-gather.2 = bf16[32,1,256]{2,1,0:T(2,128)(2,1)S(1)} all-gather(bf16[1,1,256]{2,1,0:T(2,128)(2,1)S(1)} %reshape.161), channel_id=3, replica_groups=mesh['ctx'=32,'head'=16] {'ctx'}, dimensions={0}, use_global_device_ids=true | all-gather | bytes 16896 | tf_op jit(solution)/shard_map/all_gather | solution.py:19
  130.0 41.1 %all-gather.14.cloned.1.call-done = bf16[8192,128]{1,0:T(8,128)(2,1)} async-done(((bf16[256,128]{1,0:T(8,128)(2,1)}), bf16[8192,128]{1,0:T(8,128)(2,1)}) %all-gather.14.cloned.1.call-update) | async-done | bytes 2097168 | tf_op jit(solution)/shard_map/all_gather | solution.py:19
  171.1 30.8 %while.16 = (s32[]{:T(128)}, f32[256,128]{1,0:T(8,128)S(1)}, f32[256]{0:T(256)S(1)}, s32[]{:T(128)}, bf16[32,256,128]{2,1,0:T(8,128)(2,1)}, /*index=5*/bf16[32,256]{1,0:T(8,128)(2,1)S(1)}, s32[]{:T(128)}, s32[]{:T(128)}) while((s32[]{:T(128)}, f32[256,128]{1,0:T(8,128)S(1)}, f32[256]{0:T(256)S(1)}, s32[]{:T(128)}, ...), condition=%wide.region_6.7_spmd.clone, body=%wide.region_5.6_spmd.clone.sunk | while | flops 132100 | bytes 332403 | solution.py:36
  171.1 0.9 add_select_fusion.4
  172.1 0.9 add_select_fusion.4
  173.1 0.9 add_select_fusion.4
  174.0 0.9 add_select_fusion.4
  175.0 0.9 add_select_fusion.4
  175.9 0.9 add_select_fusion.4
  176.9 0.9 add_select_fusion.4
  177.9 0.9 add_select_fusion.4
  178.8 0.9 add_select_fusion.4
  179.8 0.9 add_select_fusion.4
  180.8 0.9 add_select_fusion.4
  181.7 0.9 add_select_fusion.4
  182.7 0.9 add_select_fusion.4
  183.7 0.9 add_select_fusion.4
  184.6 0.9 add_select_fusion.4
  185.6 0.9 add_select_fusion.4
  186.6 0.9 add_select_fusion.4
  187.5 0.9 add_select_fusion.4
  188.5 0.9 add_select_fusion.4
  189.4 0.9 add_select_fusion.4
  190.4 0.9 add_select_fusion.4
  191.4 0.9 add_select_fusion.4
  192.3 0.9 add_select_fusion.4
  193.3 0.9 add_select_fusion.4
  194.3 0.9 add_select_fusion.4
  195.2 0.9 add_select_fusion.4
  196.2 0.9 add_select_fusion.4
  197.2 0.9 add_select_fusion.4
  198.1 0.9 add_select_fusion.4
  199.1 0.9 add_select_fusion.4
  200.1 0.9 add_select_fusion.4
  201.0 0.9 add_select_fusion.4
  202.0 58.0 %all-gather.8.cloned.1.call-done = bf16[16384,128]{1,0:T(8,128)(2,1)} async-done(((bf16[512,128]{1,0:T(8,128)(2,1)}), bf16[16384,128]{1,0:T(8,128)(2,1)}) %all-gather.8.cloned.1.call-update) | async-done | bytes 4194320 | tf_op jit(solution)/shard_map/all_gather | solution.py:64
  260.0 6.9 %convolution_convert_fusion.2 = bf16[256,128]{1,0:T(8,128)(2,1)S(1)} fusion(bf16[256,16384]{1,0:T(8,128)(2,1)} %param.8, bf16[16384,128]{1,0:T(8,128)(2,1)} %all-gather.8.cloned.1.call-done), kind=kOutput, calls=%fused_computation.15 | convolution fusion | flops 1073774592 | bytes 12648448 | tf_op jit(solution)/shard_map/dot_general | solution.py:62
  268.3 1.2 fusion.6
  269.5 78.3 %all-gather.12.cloned.1.call-done = bf16[2048,1024]{1,0:T(8,128)(2,1)} async-done(((bf16[64,1024]{1,0:T(8,128)(2,1)}), bf16[2048,1024]{1,0:T(8,128)(2,1)}) %all-gather.12.cloned.1.call-update) | async-done | bytes 4194320 | tf_op jit(solution)/shard_map/all_gather | solution.py:122
  347.8 43.5 %all-gather.10.cloned.1.call-done = bf16[256,2048]{1,0:T(8,128)(2,1)} async-done(((bf16[256,128]{1,0:T(8,128)(2,1)}), bf16[256,2048]{1,0:T(8,128)(2,1)}) %all-gather.10.cloned.1.call-update) | async-done | bytes 1048592 | tf_op jit(solution)/shard_map/all_gather | solution.py:118
  391.3 4.6 %convolution_convert_fusion = bf16[256,1024]{1,0:T(8,128)(2,1)} fusion(bf16[256,2048]{1,0:T(8,128)(2,1)} %all-gather.10.cloned.1.call-done, bf16[2048,1024]{1,0:T(8,128)(2,1)} %all-gather.12.cloned.1.call-done), kind=kOutput, calls=%fused_computation.3 | convolution fusion | flops 1074003968 | bytes 5767168 | tf_op jit(solution)/shard_map/dot_general | solution.py:120
  (93 shorter events, 4.0 us)
Async XLA Ops:
  6.5 84.9 %copy-start = (bf16[128,128]{1,0:T(8,128)(2,1)S(1)}, bf16[128,128]{1,0:T(8,128)(2,1)}, u32[]{:S(2)}) copy-start(bf16[128,128]{1,0:T(8,128)(2,1)} %param.12) | copy-start | bytes 98308
  6.5 164.6 %all-gather.14.cloned.1.call-start = ((), (), s32[]{:S(2)}) async-start(), calls=%async_computation.3 | async-start | bytes 2162688 | tf_op jit(solution)/shard_map/all_gather | solution.py:19
  87.7 3.7 collective-permute-start
  93.1 166.9 %all-gather.8.cloned.1.call-start = ((), (), s32[]{:S(2)}) async-start(), calls=%async_computation | async-start | bytes 4325376 | tf_op jit(solution)/shard_map/all_gather | solution.py:64
  93.9 253.9 %all-gather.12.cloned.1.call-start = ((), (), s32[]{:S(2)}) async-start(), calls=%async_computation.2 | async-start | bytes 4325376 | tf_op jit(solution)/shard_map/all_gather | solution.py:122
  94.6 296.7 %all-gather.10.cloned.1.call-start = ((), (), s32[]{:S(2)}) async-start(), calls=%async_computation.1 | async-start | bytes 1114112 | tf_op jit(solution)/shard_map/all_gather | solution.py:118
  202.0 64.9 %copy-start.1 = (bf16[1,128,128]{2,1,0:T(8,128)(2,1)S(1)}, bf16[1,128,128]{2,1,0:T(8,128)(2,1)}, u32[]{:S(2)}) copy-start(bf16[1,128,128]{2,1,0:T(8,128)(2,1)} %param.11) | copy-start | bytes 98308
Sparse Core Ops, SparseCore 0:
  93.2 77.8 all-gather.13
  174.3 85.6 all-gather.7
  263.1 84.6 all-gather.11
  349.7 41.5 all-gather.9
where the time goes:
time: 404 us; the launch traced here: 402 us
  waiting for transfers between devices  224 us (55%)
  blocking collectives  111 us (27%)
  other arithmetic  30.2 us (7%)
  matrix products  21 us (5%)
  between operations  13.3 us (3%)
    all_gather x1, waiting for transfers between devices, per_device(): lax.all_gather(w_out, 'ctx', axis=0, tiled=True)  78.3 us
    all_gather x1, waiting for transfers between devices, per_device(): lax.all_gather(w_query, 'ctx', axis=0, tiled=True)  58 us
    all_gather x1, waiting for transfers between devices, per_device(): all_heads = lax.all_gather(attn_rows, 'head', axis=1, tiled=True)  43.5 us
    all_gather x1, waiting for transfers between devices, prefix(): lax.all_gather(part.astype(kind), axis)  41.1 us
    all_gather x1, blocking collectives, per_device(): lax.all_gather(w_keyval, 'ctx', axis=0, tiled=True)  39.9 us
    all_gather x1, blocking collectives, per_device(): lax.all_gather(pair_sum.astype(jnp.bfloat16), 'head', axis=1, tiled=True)  35.5 us
    all_gather x1, blocking collectives, prefix(): lax.all_gather(part.astype(kind), axis)  35.3 us
    select_n x64, other arithmetic, step(): return jax.tree.map(lambda a, b: jnp.where(reached, a, b), new, before)  29.3 us
  transfers between devices with their start and end apart: 5, of which 5 were waited for; matrix products, arithmetic and copies ran while one was open for 10% of the time, Pallas kernels for 0%

commit v1 on v0

--- a/solution.py
+++ b/solution.py
@@ -5,6 +5,12 @@
 from jax.sharding import PartitionSpec as P
 
 WINDOW = 64
+
+
+def draw_sizes_in(target, dim_k):
+    big = jnp.stack([target for _ in range(lax.axis_size("ctx"))], axis=0)
+    latest = lax.all_to_all(big, "ctx", 0, 0)
+    return jnp.concatenate(latest, axis=dim_k)
 
 
 def from_behind(array, axis, by):
@@ -64,11 +70,7 @@
         lax.all_gather(w_query, "ctx", axis=0, tiled=True),
         preferred_element_type=jnp.float32,
     )
-    pair_sum = jnp.dot(
-        columns,
-        lax.all_gather(w_keyval, "ctx", axis=0, tiled=True),
-        preferred_element_type=jnp.float32,
-    )
+    pair_sum = jnp.dot(columns, draw_sizes_in(w_keyval, 0), preferred_element_type=jnp.float32)
     queries = query_sum.astype(jnp.bfloat16)
     keyval = lax.all_gather(pair_sum.astype(jnp.bfloat16), "head", axis=1, tiled=True)
     border = from_behind(keyval[length - WINDOW :], "ctx", 1)

time: 404 us -> 380 us (0.941)
  blocking collectives: 111 us -> 59 us
  waiting for transfers between devices: 224 us -> 239 us
  starting transfers between devices: 2.53 us -> 13.2 us
    all_gather x1 -> x0, blocking collectives: 39.9 us -> none  [per_device(): lax.all_gather(w_keyval, 'ctx', axis=0, tiled=True)]
    all_to_all x0 -> x1, waiting for transfers between devices: none -> 16.2 us  [draw_sizes_in(): latest = lax.all_to_all(big, 'ctx', 0, 0)]
    all_to_all x0 -> x1, starting transfers between devices: none -> 10.5 us  [draw_sizes_in(): latest = lax.all_to_all(big, 'ctx', 0, 0)]
    all_gather x1, blocking collectives: 35.5 us -> 25.7 us  [per_device(): lax.all_gather(pair_sum.astype(jnp.bfloat16), 'head', axis=1, tiled=True)]
  transfers between devices with their start and end apart: 5 -> 6, of which waited for: 5 -> 6; matrix products, arithmetic and copies ran while one was open for 10% -> 10% of each run, Pallas kernels for 0% -> 0%
where the time goes in v1:
time: 380 us; the launch traced here: 379 us
  waiting for transfers between devices  239 us (63%)
  blocking collectives  59 us (16%)
  other arithmetic  30.2 us (8%)
  matrix products  21 us (6%)
  between operations  13.3 us (4%)
  starting transfers between devices  13.2 us (3%)
    all_gather x1, waiting for transfers between devices, per_device(): lax.all_gather(w_out, 'ctx', axis=0, tiled=True)  78.3 us
    all_gather x1, waiting for transfers between devices, per_device(): lax.all_gather(w_query, 'ctx', axis=0, tiled=True)  58 us
    all_gather x1, waiting for transfers between devices, per_device(): all_heads = lax.all_gather(attn_rows, 'head', axis=1, tiled=True)  43.5 us
    all_gather x1, waiting for transfers between devices, prefix(): lax.all_gather(part.astype(kind), axis)  40.6 us
    all_gather x1, blocking collectives, prefix(): lax.all_gather(part.astype(kind), axis)  33.3 us
    select_n x64, other arithmetic, step(): return jax.tree.map(lambda a, b: jnp.where(reached, a, b), new, before)  29.3 us
    all_gather x1, blocking collectives, per_device(): lax.all_gather(pair_sum.astype(jnp.bfloat16), 'head', axis=1, tiled=True)  25.7 us
    all_to_all x1, waiting for transfers between devices, draw_sizes_in(): latest = lax.all_to_all(big, 'ctx', 0, 0)  16.2 us
  transfers between devices with their start and end apart: 6, of which 6 were waited for; matrix products, arithmetic and copies ran while one was open for 10% of the time, Pallas kernels for 0%

profile of v1, /device:TPU:1, one launch (start us, length us, event | category | flops | bytes accessed | tf_op | source)
XLA Modules:
  0.0 378.6 jit_solution(11672189682209694633)
XLA Ops:
  6.5 1.6 stack.2
  8.1 10.5 %all-to-all-start = ((bf16[32,512,16]{1,2,0:T(8,128)(2,1)}), bf16[32,512,16]{1,2,0:T(8,128)(2,1)S(1)}, u32[]{:S(2)}, u32[]{:S(2)}) async-start(bf16[32,512,16]{1,2,0:T(8,128)(2,1)} %stack.2), calls=%async_computation | async-start | bytes 1048576 | tf_op jit(solution)/shard_map/all_to_all | solution.py:12
  18.7 16.2 %all-to-all-done = bf16[32,512,16]{1,2,0:T(8,128)(2,1)S(1)} async-done(((bf16[32,512,16]{1,2,0:T(8,128)(2,1)}), bf16[32,512,16]{1,2,0:T(8,128)(2,1)S(1)}, u32[]{:S(2)}, u32[]{:S(2)}) %all-to-all-start) | async-done | bytes 524320 | tf_op jit(solution)/shard_map/all_to_all | solution.py:12
  34.9 5.6 %convolution_convert_fusion.3 = bf16[256,16]{0,1:T(8,128)(2,1)S(1)} fusion(bf16[256,16384]{1,0:T(8,128)(2,1)} %param.8, bf16[16384,16]{0,1:T(8,128)(2,1)S(1)} %bitcast.45), kind=kOutput, calls=%fused_computation.16 | convolution fusion | flops 134221824 | bytes 8921088 | tf_op jit(solution)/shard_map/dot_general | solution.py:73
  40.6 25.7 %all_gather.24 = bf16[256,256]{0,1:T(8,128)(2,1)S(1)} all-gather(bf16[256,16]{0,1:T(8,128)(2,1)S(1)} %convolution_convert_fusion.3), channel_id=1, replica_groups=mesh['ctx'=32,'head'=16] {'head'}, dimensions={1}, use_global_device_ids=true | all-gather | bytes 139264 | tf_op jit(solution)/shard_map/all_gather | solution.py:75
  66.4 2.5 collective-permute-start
  69.0 1.3 collective-permute-done
  73.6 33.3 %all-gather.2 = bf16[32,1,256]{2,1,0:T(2,128)(2,1)S(1)} all-gather(bf16[1,1,256]{2,1,0:T(2,128)(2,1)S(1)} %reshape.167), channel_id=3, replica_groups=mesh['ctx'=32,'head'=16] {'ctx'}, dimensions={0}, use_global_device_ids=true | all-gather | bytes 16896 | tf_op jit(solution)/shard_map/all_gather | solution.py:25
  106.9 40.6 %all-gather.14.cloned.1.call-done = bf16[8192,128]{1,0:T(8,128)(2,1)} async-done(((bf16[256,128]{1,0:T(8,128)(2,1)}), bf16[8192,128]{1,0:T(8,128)(2,1)}) %all-gather.14.cloned.1.call-update) | async-done | bytes 2097168 | tf_op jit(solution)/shard_map/all_gather | solution.py:25
  147.4 30.8 %while.16 = (s32[]{:T(128)}, f32[256,128]{1,0:T(8,128)S(1)}, f32[256]{0:T(256)S(1)}, s32[]{:T(128)}, bf16[32,256,128]{2,1,0:T(8,128)(2,1)}, /*index=5*/bf16[32,256]{1,0:T(8,128)(2,1)S(1)}, s32[]{:T(128)}, s32[]{:T(128)}) while((s32[]{:T(128)}, f32[256,128]{1,0:T(8,128)S(1)}, f32[256]{0:T(256)S(1)}, s32[]{:T(128)}, ...), condition=%wide.region_6.7_spmd.clone, body=%wide.region_5.6_spmd.clone.sunk | while | flops 132100 | bytes 332403 | solution.py:42
  147.4 0.9 add_select_fusion.4
  148.4 0.9 add_select_fusion.4
  149.3 0.9 add_select_fusion.4
  150.3 0.9 add_select_fusion.4
  151.3 0.9 add_select_fusion.4
  152.2 0.9 add_select_fusion.4
  153.2 0.9 add_select_fusion.4
  154.2 0.9 add_select_fusion.4
  155.1 0.9 add_select_fusion.4
  156.1 0.9 add_select_fusion.4
  157.1 0.9 add_select_fusion.4
  158.0 0.9 add_select_fusion.4
  159.0 0.9 add_select_fusion.4
  159.9 0.9 add_select_fusion.4
  160.9 0.9 add_select_fusion.4
  161.9 0.9 add_select_fusion.4
  162.8 0.9 add_select_fusion.4
  163.8 0.9 add_select_fusion.4
  164.8 0.9 add_select_fusion.4
  165.7 0.9 add_select_fusion.4
  166.7 0.9 add_select_fusion.4
  167.7 0.9 add_select_fusion.4
  168.6 0.9 add_select_fusion.4
  169.6 0.9 add_select_fusion.4
  170.6 0.9 add_select_fusion.4
  171.5 0.9 add_select_fusion.4
  172.5 0.9 add_select_fusion.4
  173.4 0.9 add_select_fusion.4
  174.4 0.9 add_select_fusion.4
  175.4 0.9 add_select_fusion.4
  176.3 0.9 add_select_fusion.4
  177.3 0.9 add_select_fusion.4
  178.3 58.0 %all-gather.8.cloned.1.call-done = bf16[16384,128]{1,0:T(8,128)(2,1)} async-done(((bf16[512,128]{1,0:T(8,128)(2,1)}), bf16[16384,128]{1,0:T(8,128)(2,1)}) %all-gather.8.cloned.1.call-update) | async-done | bytes 4194320 | tf_op jit(solution)/shard_map/all_gather | solution.py:70
  236.3 6.9 %convolution_convert_fusion.2 = bf16[256,128]{1,0:T(8,128)(2,1)S(1)} fusion(bf16[256,16384]{1,0:T(8,128)(2,1)} %param.8, bf16[16384,128]{1,0:T(8,128)(2,1)} %all-gather.8.cloned.1.call-done), kind=kOutput, calls=%fused_computation.15 | convolution fusion | flops 1073774592 | bytes 12648448 | tf_op jit(solution)/shard_map/dot_general | solution.py:68
  244.6 1.2 fusion.6
  245.8 78.3 %all-gather.12.cloned.1.call-done = bf16[2048,1024]{1,0:T(8,128)(2,1)} async-done(((bf16[64,1024]{1,0:T(8,128)(2,1)}), bf16[2048,1024]{1,0:T(8,128)(2,1)}) %all-gather.12.cloned.1.call-update) | async-done | bytes 4194320 | tf_op jit(solution)/shard_map/all_gather | solution.py:124
  324.1 43.5 %all-gather.10.cloned.1.call-done = bf16[256,2048]{1,0:T(8,128)(2,1)} async-done(((bf16[256,128]{1,0:T(8,128)(2,1)}), bf16[256,2048]{1,0:T(8,128)(2,1)}) %all-gather.10.cloned.1.call-update) | async-done | bytes 1048592 | tf_op jit(solution)/shard_map/all_gather | solution.py:120
  367.5 4.6 %convolution_convert_fusion = bf16[256,1024]{1,0:T(8,128)(2,1)} fusion(bf16[256,2048]{1,0:T(8,128)(2,1)} %all-gather.10.cloned.1.call-done, bf16[2048,1024]{1,0:T(8,128)(2,1)} %all-gather.12.cloned.1.call-done), kind=kOutput, calls=%fused_computation.3 | convolution fusion | flops 1074003968 | bytes 5767168 | tf_op jit(solution)/shard_map/dot_general | solution.py:122
  (96 shorter events, 5.7 us)
Async XLA Ops:
  6.5 63.7 %copy-start = (bf16[128,128]{1,0:T(8,128)(2,1)S(1)}, bf16[128,128]{1,0:T(8,128)(2,1)}, u32[]{:S(2)}) copy-start(bf16[128,128]{1,0:T(8,128)(2,1)} %param.12) | copy-start | bytes 98308
  8.1 26.8 %all-to-all-start = ((bf16[32,512,16]{1,2,0:T(8,128)(2,1)}), bf16[32,512,16]{1,2,0:T(8,128)(2,1)S(1)}, u32[]{:S(2)}, u32[]{:S(2)}) async-start(bf16[32,512,16]{1,2,0:T(8,128)(2,1)} %stack.2), calls=%async_computation | async-start | bytes 1048576 | tf_op jit(solution)/shard_map/all_to_all | solution.py:12
  18.6 128.8 %all-gather.14.cloned.1.call-start = ((), (), s32[]{:S(2)}) async-start(), calls=%async_computation.4 | async-start | bytes 2162688 | tf_op jit(solution)/shard_map/all_gather | solution.py:25
  66.4 3.9 %collective-permute-start = (bf16[64,256]{0,1:T(8,128)(2,1)S(1)}, bf16[64,256]{0,1:T(8,128)(2,1)S(1)}, u32[]{:S(2)}, u32[]{:S(2)}) collective-permute-start(bf16[64,256]{0,1:T(8,128)(2,1)S(1)} %slice.21), channel_id=1, source_target_pairs={{0,16},{16,32},{32,48},{48,64},{64,80},{80,96},{96,112},{112,128},... | collective-permute-start | bytes 98312 | tf_op jit(solution)/shard_map/ppermute | solution.py:19
  71.9 164.3 %all-gather.8.cloned.1.call-start = ((), (), s32[]{:S(2)}) async-start(), calls=%async_computation.1 | async-start | bytes 4325376 | tf_op jit(solution)/shard_map/all_gather | solution.py:70
  72.7 251.4 %all-gather.12.cloned.1.call-start = ((), (), s32[]{:S(2)}) async-start(), calls=%async_computation.3 | async-start | bytes 4325376 | tf_op jit(solution)/shard_map/all_gather | solution.py:124
  73.4 294.1 %all-gather.10.cloned.1.call-start = ((), (), s32[]{:S(2)}) async-start(), calls=%async_computation.2 | async-start | bytes 1114112 | tf_op jit(solution)/shard_map/all_gather | solution.py:120
  178.2 64.9 %copy-start.1 = (bf16[1,128,128]{2,1,0:T(8,128)(2,1)S(1)}, bf16[1,128,128]{2,1,0:T(8,128)(2,1)}, u32[]{:S(2)}) copy-start(bf16[1,128,128]{2,1,0:T(8,128)(2,1)} %param.11) | copy-start | bytes 98308
Sparse Core Ops, SparseCore 0:
  72.1 75.3 all-gather.13
  150.6 85.6 all-gather.7
  239.4 84.6 all-gather.11
  326.0 41.5 all-gather.9
